TPU v7x, 32 devices: a whole 2x2x4 slice. The times are simulated.
32 devices in a mesh: dp: 8 (over z, y), ctx: 4 (over x, core).
Axes of the slice: x: 2, y: 2, z: 4, core: 2. Of those that a mesh axis runs over, the one named last changes fastest.
Arguments:
- tokens: bfloat16 [8, 1024, 2048], P('dp', 'ctx'), may hold values from -6 to 6
- cotangent: bfloat16 [8, 1024, 2048], P('dp', 'ctx'), may hold values from -6 to 6
- domain_ids: int32 [8], P('dp'), may hold values from 0 to 31
- domain_counts: int32 [32], replicated, may hold values from 1024 to 4096
- domain_numer: int32 [32], replicated, may hold values from 1 to 8
- domain_denom: int32 [32], replicated, may hold values from 1 to 8
- attention_gain: bfloat16 [2048], replicated, may hold values from 0.5 to 1.5
- query_gain: bfloat16 [128], replicated, may hold values from 0.796875 to 1.796875
- key_gain: bfloat16 [128], replicated, may hold values from 0.796875 to 1.796875
- query_proj: bfloat16 [2048, 2048], P('dp', 'ctx'), may hold values from -0.125 to 0.125
- key_proj: bfloat16 [2048, 1024], P('dp', 'ctx'), may hold values from -0.125 to 0.125
- value_proj: bfloat16 [2048, 1024], P('dp', 'ctx'), may hold values from -0.125 to 0.125
- gating_proj: bfloat16 [2048, 2048], P('dp', 'ctx'), may hold values from -0.125 to 0.125
- output_proj: bfloat16 [2048, 2048], P('ctx', 'dp'), may hold values from -1 to 1
- swiglu_gain: bfloat16 [2048], replicated, may hold values from 0.5 to 1.5
- swiglu_gate: bfloat16 [2048, 6144], P('dp', 'ctx'), may hold values from -0.125 to 0.125
- swiglu_up: bfloat16 [2048, 6144], P('dp', 'ctx'), may hold values from -0.125 to 0.125
- swiglu_down: bfloat16 [6144, 2048], P('ctx', 'dp'), may hold values from -0.109375 to 0.109375
Outputs:
- layer_out: bfloat16 [8, 1024, 2048], P('dp', 'ctx')
- input_grad: bfloat16 [8, 1024, 2048], P('dp', 'ctx')
- attention_gain_grad: float32 [2048], replicated
- query_gain_grad: float32 [128], replicated
- key_gain_grad: float32 [128], replicated
- query_proj_grad: float32 [2048, 2048], P('dp', 'ctx')
- key_proj_grad: float32 [2048, 1024], P('dp', 'ctx')
- value_proj_grad: float32 [2048, 1024], P('dp', 'ctx')
- gating_proj_grad: float32 [2048, 2048], P('dp', 'ctx')
- output_proj_grad: float32 [2048, 2048], P('ctx', 'dp')
- swiglu_gain_grad: float32 [2048], replicated
- swiglu_gate_grad: float32 [2048, 6144], P('dp', 'ctx')
- swiglu_up_grad: float32 [2048, 6144], P('dp', 'ctx')
- swiglu_down_grad: float32 [6144, 2048], P('ctx', 'dp')
All inputs are finite; a program needn't handle non-finite values.
Results may differ from a plain program's by a relative error of at most 0.019.
Values may be sent and summed in bfloat16 or wider, within the bound.
A program may use at most 192 MiB of HBM per device.

v0:
```python
import jax
import jax.numpy as jnp
from jax import lax
from jax.sharding import PartitionSpec as P

LENGTH = 1024
EPSILON = 1e-06
ROPE_BASE = 1000000.0


def matmul_f32(left, right):
    return jnp.dot(left, right, preferred_element_type=jnp.float32)


def matmul_tn(left, right):
    return lax.dot_general(
        left, right, (((0,), (0,)), ((), ())), preferred_element_type=jnp.float32
    )


def matmul_nt(left, right):
    return lax.dot_general(
        left, right, (((1,), (1,)), ((), ())), preferred_element_type=jnp.float32
    )


def rope_tables(positions, head_width):
    halfway = head_width // 2
    inverse = 1.0 / ROPE_BASE ** (jnp.arange(halfway, dtype=jnp.float32) * (2.0 / head_width))
    angles = positions.astype(jnp.float32)[:, None] * inverse[None, :]
    return (jnp.cos(angles), jnp.sin(angles))


def rotate(tensor, cosine, sine):
    halfway = tensor.shape[-1] // 2
    first_half = tensor[..., :halfway]
    second_half = tensor[..., halfway:]
    return jnp.concatenate(
        [first_half * cosine - second_half * sine, second_half * cosine + first_half * sine], -1
    )


def unrotate(grads_in, cosine, sine):
    halfway = grads_in.shape[-1] // 2
    first_half = grads_in[..., :halfway]
    second_half = grads_in[..., halfway:]
    return jnp.concatenate(
        [first_half * cosine + second_half * sine, second_half * cosine - first_half * sine], -1
    )


def norm_back(grads_in, values_in, inverse, gain_vec):
    scaled = grads_in * gain_vec
    return inverse * scaled - values_in * (inverse * inverse * inverse) * jnp.mean(
        scaled * values_in, -1, keepdims=True
    )


def attention_weights(query_proj, key_proj, value_proj, gating_proj, output_proj):
    return (
        lax.all_gather(query_proj, "dp", axis=0, tiled=True),
        lax.all_gather(key_proj, "dp", axis=0, tiled=True),
        lax.all_gather(value_proj, "dp", axis=0, tiled=True),
        lax.all_gather(gating_proj, "dp", axis=0, tiled=True),
        lax.all_gather(output_proj, "dp", axis=1, tiled=True),
    )


def swiglu_weights(swiglu_gate, swiglu_up, swiglu_down):
    return (
        lax.all_gather(swiglu_gate, "dp", axis=0, tiled=True),
        lax.all_gather(swiglu_up, "dp", axis=0, tiled=True),
        lax.all_gather(swiglu_down, "dp", axis=1, tiled=True),
    )


def softmax_forward(seq_items, causal):
    queries, keys_seq, values_seq = seq_items
    scaling = queries.shape[-1] ** (-0.5)
    scores = (
        jnp.einsum("qgjd,kgd->gjqk", queries, keys_seq, preferred_element_type=jnp.float32)
        * scaling
    )
    scores = jnp.where(causal, scores, -1e30)
    highest = jnp.max(scores, -1, keepdims=True)
    exp_vals = jnp.exp(scores - highest)
    row_totals = jnp.sum(exp_vals, -1, keepdims=True)
    attn_probs = (exp_vals / row_totals).astype(jnp.bfloat16)
    attended = jnp.einsum(
        "gjqk,kgd->qgjd", attn_probs, values_seq, preferred_element_type=jnp.float32
    )
    return (attended, highest[..., 0] + jnp.log(row_totals[..., 0]))


def softmax_backward(seq_items, causal):
    queries, keys_seq, values_seq, log_total, upstream = seq_items
    scaling = queries.shape[-1] ** (-0.5)
    scores = (
        jnp.einsum("qgjd,kgd->gjqk", queries, keys_seq, preferred_element_type=jnp.float32)
        * scaling
    )
    scores = jnp.where(causal, scores, -1e30)
    attn_probs = jnp.exp(scores - log_total[..., None])
    dprobs = jnp.einsum("qgjd,kgd->gjqk", upstream, values_seq, preferred_element_type=jnp.float32)
    centre = jnp.sum(dprobs * attn_probs, -1, keepdims=True)
    dscores = (attn_probs * (dprobs - centre)).astype(jnp.bfloat16)
    dqueries = (
        jnp.einsum("gjqk,kgd->qgjd", dscores, keys_seq, preferred_element_type=jnp.float32)
        * scaling
    )
    key_grads = (
        jnp.einsum("gjqk,qgjd->kgd", dscores, queries, preferred_element_type=jnp.float32) * scaling
    )
    value_grads = jnp.einsum(
        "gjqk,qgjd->kgd",
        attn_probs.astype(jnp.bfloat16),
        upstream,
        preferred_element_type=jnp.float32,
    )
    key_rows = key_grads.shape[0]
    return (dqueries, key_grads.reshape(key_rows, -1), value_grads.reshape(key_rows, -1))


def per_device(
    tokens,
    cotangent,
    domain_ids,
    domain_counts,
    domain_numer,
    domain_denom,
    attention_gain,
    query_gain,
    key_gain,
    query_proj,
    key_proj,
    value_proj,
    gating_proj,
    output_proj,
    swiglu_gain,
    swiglu_gate,
    swiglu_up,
    swiglu_down,
):
    seq_count, local_len, model_width = tokens.shape
    full_len = local_len * lax.axis_size("ctx")
    local_rows = seq_count * local_len
    all_rows = seq_count * full_len
    head_dim = query_gain.shape[0]
    local_heads = query_proj.shape[1] // head_dim
    local_kv = key_proj.shape[1] // head_dim
    group_size = local_heads // local_kv
    positions = jnp.arange(full_len, dtype=jnp.int32)
    causal = positions[:, None] >= positions[None, :]
    cosine, sine = rope_tables(positions, head_dim)
    cos_rows = cosine[:, None, :]
    sin_rows = sine[:, None, :]
    inputs = tokens.reshape(local_rows, model_width).astype(jnp.float32)
    inverse_in = lax.rsqrt(jnp.mean(inputs * inputs, -1, keepdims=True) + EPSILON)
    gain_in = attention_gain.astype(jnp.float32)
    normed = (inputs * inverse_in * gain_in).astype(jnp.bfloat16)
    normed_all = lax.all_gather(
        normed.reshape(seq_count, local_len, model_width), "ctx", axis=1, tiled=True
    ).reshape(all_rows, model_width)
    attn_full = attention_weights(query_proj, key_proj, value_proj, gating_proj, output_proj)
    query_raw = matmul_f32(normed_all, attn_full[0]).reshape(
        seq_count, full_len, local_heads, head_dim
    )
    key_raw = matmul_f32(normed_all, attn_full[1]).reshape(seq_count, full_len, local_kv, head_dim)
    value_low = (
        matmul_f32(normed_all, attn_full[2])
        .astype(jnp.bfloat16)
        .reshape(seq_count, full_len, local_kv, head_dim)
    )
    gate_pre = matmul_f32(normed_all, attn_full[3])
    query_scale = query_gain.astype(jnp.float32)
    key_scale = key_gain.astype(jnp.float32)
    query_inv = lax.rsqrt(jnp.mean(query_raw * query_raw, -1, keepdims=True) + EPSILON)
    key_inv = lax.rsqrt(jnp.mean(key_raw * key_raw, -1, keepdims=True) + EPSILON)
    query_low = rotate(query_raw * query_inv * query_scale, cos_rows, sin_rows).astype(jnp.bfloat16)
    key_low = rotate(key_raw * key_inv * key_scale, cos_rows, sin_rows).astype(jnp.bfloat16)
    query_groups = query_low.reshape(seq_count, full_len, local_kv, group_size, head_dim)
    attended, log_total = lax.map(
        lambda seq_items: softmax_forward(seq_items, causal), (query_groups, key_low, value_low)
    )
    attended = attended.reshape(all_rows, local_heads * head_dim)
    gate_sig = jax.nn.sigmoid(gate_pre)
    mixed = (attended * gate_sig).astype(jnp.bfloat16)
    branch_part = matmul_f32(mixed, attn_full[4]).reshape(seq_count, full_len, model_width)
    branch = lax.psum_scatter(branch_part, "ctx", scatter_dimension=1, tiled=True).reshape(
        local_rows, model_width
    )
    hidden = inputs + branch
    inverse_mid = lax.rsqrt(jnp.mean(hidden * hidden, -1, keepdims=True) + EPSILON)
    gain_mid = swiglu_gain.astype(jnp.float32)
    normed_mid = (hidden * inverse_mid * gain_mid).astype(jnp.bfloat16)
    normed_mid_all = lax.all_gather(
        normed_mid.reshape(seq_count, local_len, model_width), "ctx", axis=1, tiled=True
    ).reshape(all_rows, model_width)
    swiglu_full = swiglu_weights(swiglu_gate, swiglu_up, swiglu_down)
    gate_ff = matmul_f32(normed_mid_all, swiglu_full[0])
    up_val = matmul_f32(normed_mid_all, swiglu_full[1])
    gate_sigma = jax.nn.sigmoid(gate_ff)
    silu_val = gate_ff * gate_sigma
    activation = (silu_val * up_val).astype(jnp.bfloat16)
    down_part = matmul_f32(activation, swiglu_full[2]).reshape(seq_count, full_len, model_width)
    ffn_branch = (
        lax.psum_scatter(down_part.astype(jnp.bfloat16), "ctx", scatter_dimension=1, tiled=True)
        .astype(jnp.float32)
        .reshape(local_rows, model_width)
    )
    layer_out = (hidden + ffn_branch).astype(jnp.bfloat16)
    domain_table = (
        domain_ids[:, None] == jnp.arange(domain_counts.shape[0], dtype=jnp.int32)[None, :]
    ).astype(jnp.float32)
    ratio = (
        domain_numer.astype(jnp.float32)
        / domain_denom.astype(jnp.float32)
        * LENGTH
        / domain_counts.astype(jnp.float32)
    )
    factor = jnp.sum(domain_table * ratio[None, :], 1)
    upstream = (cotangent.astype(jnp.float32) * factor[:, None, None]).reshape(
        local_rows, model_width
    )
    swiglu_back = swiglu_weights(swiglu_gate, swiglu_up, swiglu_down)
    out_low = upstream.astype(jnp.bfloat16)
    out_all = lax.all_gather(
        out_low.reshape(seq_count, local_len, model_width), "ctx", axis=1, tiled=True
    ).reshape(all_rows, model_width)
    dactivation = matmul_nt(out_all, swiglu_back[2])
    dgate_low = (dactivation * up_val * gate_sigma * (1.0 + gate_ff * (1.0 - gate_sigma))).astype(
        jnp.bfloat16
    )
    dup_low = (dactivation * silu_val).astype(jnp.bfloat16)
    grad_down = matmul_tn(activation, out_all)
    grad_gate = matmul_tn(normed_mid_all, dgate_low)
    grad_up = matmul_tn(normed_mid_all, dup_low)
    dmid_part = matmul_nt(dgate_low, swiglu_back[0]) + matmul_nt(dup_low, swiglu_back[1])
    dnormed_mid = lax.psum_scatter(
        dmid_part.reshape(seq_count, full_len, model_width), "ctx", scatter_dimension=1, tiled=True
    ).reshape(local_rows, model_width)
    grad_gain_mid = jnp.sum(dnormed_mid * hidden * inverse_mid, 0)
    dhidden = upstream + norm_back(dnormed_mid, hidden, inverse_mid, gain_mid)
    swiglu_grads = (
        lax.psum_scatter(
            grad_gate.astype(jnp.bfloat16), "dp", scatter_dimension=0, tiled=True
        ).astype(jnp.float32),
        lax.psum_scatter(
            grad_up.astype(jnp.bfloat16), "dp", scatter_dimension=0, tiled=True
        ).astype(jnp.float32),
        lax.psum_scatter(
            grad_down.astype(jnp.bfloat16), "dp", scatter_dimension=1, tiled=True
        ).astype(jnp.float32),
    )
    attn_back = attention_weights(query_proj, key_proj, value_proj, gating_proj, output_proj)
    dbranch_low = dhidden.astype(jnp.bfloat16)
    dbranch_all = lax.all_gather(
        dbranch_low.reshape(seq_count, local_len, model_width), "ctx", axis=1, tiled=True
    ).reshape(all_rows, model_width)
    grad_output = matmul_tn(mixed, dbranch_all)
    dmixed = matmul_nt(dbranch_all, attn_back[4])
    dattended_low = (dmixed * gate_sig).astype(jnp.bfloat16)
    dgating_low = (dmixed * attended * gate_sig * (1.0 - gate_sig)).astype(jnp.bfloat16)
    upstream_heads = dattended_low.reshape(seq_count, full_len, local_kv, group_size, head_dim)
    dquery_rot, dkey_rot, dvalue_sum = lax.map(
        lambda seq_items: softmax_backward(seq_items, causal),
        (query_groups, key_low, value_low, log_total, upstream_heads),
    )
    dvalue_low = dvalue_sum.reshape(all_rows, local_kv * head_dim).astype(jnp.bfloat16)
    dquery_normed = unrotate(
        dquery_rot.reshape(seq_count, full_len, local_heads, head_dim), cos_rows, sin_rows
    )
    dkey_normed = unrotate(
        dkey_rot.reshape(seq_count, full_len, local_kv, head_dim), cos_rows, sin_rows
    )
    grad_query_gain = jnp.sum(dquery_normed * query_raw * query_inv, (0, 1, 2))
    grad_key_gain = jnp.sum(dkey_normed * key_raw * key_inv, (0, 1, 2))
    dquery_low = (
        norm_back(dquery_normed, query_raw, query_inv, query_scale)
        .reshape(all_rows, -1)
        .astype(jnp.bfloat16)
    )
    dkey_low = (
        norm_back(dkey_normed, key_raw, key_inv, key_scale)
        .reshape(all_rows, -1)
        .astype(jnp.bfloat16)
    )
    dnormed_part = (
        matmul_nt(dquery_low, attn_back[0])
        + matmul_nt(dkey_low, attn_back[1])
        + matmul_nt(dvalue_low, attn_back[2])
        + matmul_nt(dgating_low, attn_back[3])
    )
    dnormed = (
        lax.psum_scatter(
            dnormed_part.reshape(seq_count, full_len, model_width).astype(jnp.bfloat16),
            "ctx",
            scatter_dimension=1,
            tiled=True,
        )
        .astype(jnp.float32)
        .reshape(local_rows, model_width)
    )
    grad_gain_in = jnp.sum(dnormed * inputs * inverse_in, 0)
    input_grad = (dhidden + norm_back(dnormed, inputs, inverse_in, gain_in)).astype(jnp.bfloat16)
    grad_query = matmul_tn(normed_all, dquery_low)
    grad_key = matmul_tn(normed_all, dkey_low)
    grad_value = matmul_tn(normed_all, dvalue_low)
    grad_gating = matmul_tn(normed_all, dgating_low)
    attention_grads = (
        lax.psum_scatter(
            grad_query.astype(jnp.bfloat16), "dp", scatter_dimension=0, tiled=True
        ).astype(jnp.float32),
        lax.psum_scatter(
            grad_key.astype(jnp.bfloat16), "dp", scatter_dimension=0, tiled=True
        ).astype(jnp.float32),
        lax.psum_scatter(
            grad_value.astype(jnp.bfloat16), "dp", scatter_dimension=0, tiled=True
        ).astype(jnp.float32),
        lax.psum_scatter(
            grad_gating.astype(jnp.bfloat16), "dp", scatter_dimension=0, tiled=True
        ).astype(jnp.float32),
        lax.psum_scatter(
            grad_output.astype(jnp.bfloat16), "dp", scatter_dimension=1, tiled=True
        ).astype(jnp.float32),
    )
    gain_grads = lax.psum(
        (grad_gain_in, grad_gain_mid, grad_query_gain, grad_key_gain), ("dp", "ctx")
    )
    return (
        layer_out.reshape(seq_count, local_len, model_width),
        input_grad.reshape(seq_count, local_len, model_width),
        gain_grads[0],
        gain_grads[2],
        gain_grads[3],
        attention_grads[0],
        attention_grads[1],
        attention_grads[2],
        attention_grads[3],
        attention_grads[4],
        gain_grads[1],
        swiglu_grads[0],
        swiglu_grads[1],
        swiglu_grads[2],
    )


def solution(mesh):
    return jax.shard_map(
        per_device,
        mesh=mesh,
        in_specs=(
            P("dp", "ctx", None),
            P("dp", "ctx", None),
            P("dp"),
            P(),
            P(),
            P(),
            P(),
            P(),
            P(),
            P("dp", "ctx"),
            P("dp", "ctx"),
            P("dp", "ctx"),
            P("dp", "ctx"),
            P("ctx", "dp"),
            P(),
            P("dp", "ctx"),
            P("dp", "ctx"),
            P("ctx", "dp"),
        ),
        out_specs=(
            P("dp", "ctx", None),
            P("dp", "ctx", None),
            P(),
            P(),
            P(),
            P("dp", "ctx"),
            P("dp", "ctx"),
            P("dp", "ctx"),
            P("dp", "ctx"),
            P("ctx", "dp"),
            P(),
            P("dp", "ctx"),
            P("dp", "ctx"),
            P("ctx", "dp"),
        ),
        check_vma=False,
    )
```

profile of v0, /device:TPU:0, one launch (start us, length us, event | category | flops | bytes accessed | tf_op | source)
XLA Modules:
  0.0 1734.3 jit_solution(1612069383806065240)
XLA Ops:
  18.6 34.5 %all-gather.17.cloned.1.call-done = bf16[2048,256]{1,0:T(8,128)(2,1)} async-done(((bf16[256,256]{1,0:T(8,128)(2,1)}), bf16[2048,256]{1,0:T(8,128)(2,1)}) %all-gather.17.cloned.1.call-update) | async-done | bytes 1048592 | tf_op jit(solution)/shard_map/all_gather | solution.py:62
  53.1 35.4 %all-gather.13.cloned.1.call-done = bf16[1,1024,2048]{2,1,0:T(8,128)(2,1)} async-done(((bf16[1,256,2048]{2,1,0:T(8,128)(2,1)}), bf16[1,1024,2048]{2,1,0:T(8,128)(2,1)}) %all-gather.13.cloned.1.call-update) | async-done | bytes 4194320 | tf_op jit(solution)/shard_map/all_gather | solution.py:161
  93.4 46.5 %all-gather.19.cloned.1.call-done = bf16[2048,512]{1,0:T(8,128)(2,1)} async-done(((bf16[256,512]{1,0:T(8,128)(2,1)}), bf16[2048,512]{1,0:T(8,128)(2,1)}) %all-gather.19.cloned.1.call-update) | async-done | bytes 2097168 | tf_op jit(solution)/shard_map/all_gather | solution.py:61
  162.1 18.5 %all-gather.15.cloned.1.call-done = bf16[2048,256]{1,0:T(8,128)(2,1)} async-done(((bf16[256,256]{1,0:T(8,128)(2,1)}), bf16[2048,256]{1,0:T(8,128)(2,1)}) %all-gather.15.cloned.1.call-update) | async-done | bytes 1048592 | tf_op jit(solution)/shard_map/all_gather | solution.py:63
  200.4 30.3 %all-gather.21.cloned.1.call-done = bf16[2048,512]{1,0:T(8,128)(2,1)} async-done(((bf16[256,512]{1,0:T(8,128)(2,1)}), bf16[2048,512]{1,0:T(8,128)(2,1)}) %all-gather.21.cloned.1.call-update) | async-done | bytes 2097168 | tf_op jit(solution)/shard_map/all_gather | solution.py:64
  237.5 44.6 %all-gather.23.cloned.1.call-done = bf16[512,2048]{1,0:T(8,128)(2,1)} async-done(((bf16[512,256]{1,0:T(8,128)(2,1)}), bf16[512,2048]{1,0:T(8,128)(2,1)}) %all-gather.23.cloned.1.call-update) | async-done | bytes 2097168 | tf_op jit(solution)/shard_map/all_gather | solution.py:65
  290.3 69.2 %reduce-scatter.13.cloned.1.call-done = f32[1,256,2048]{2,1,0:T(8,128)} async-done(((f32[1,1024,2048]{2,1,0:T(8,128)}), f32[1,256,2048]{2,1,0:T(8,128)}) %reduce-scatter.13.cloned.1.call-update) | async-done | bytes 2097168 | tf_op jit(solution)/shard_map/reduce_scatter | solution.py:189
  368.7 92.3 %all-gather.29.cloned.1.call-done = bf16[2048,1536]{1,0:T(8,128)(2,1)} async-done(((bf16[256,1536]{1,0:T(8,128)(2,1)}), bf16[2048,1536]{1,0:T(8,128)(2,1)}) %all-gather.29.cloned.1.call-update) | async-done | bytes 6291472 | tf_op jit(solution)/shard_map/all_gather | solution.py:72
  461.0 34.9 %all-gather.25.cloned.1.call-done = bf16[1,1024,2048]{2,1,0:T(8,128)(2,1)} async-done(((bf16[1,256,2048]{2,1,0:T(8,128)(2,1)}), bf16[1,1024,2048]{2,1,0:T(8,128)(2,1)}) %all-gather.25.cloned.1.call-update) | async-done | bytes 4194320 | tf_op jit(solution)/shard_map/all_gather | solution.py:196
  507.7 89.6 %all-gather.27.cloned.1.call-done = bf16[2048,1536]{1,0:T(8,128)(2,1)} async-done(((bf16[256,1536]{1,0:T(8,128)(2,1)}), bf16[2048,1536]{1,0:T(8,128)(2,1)}) %all-gather.27.cloned.1.call-update) | async-done | bytes 6291472 | tf_op jit(solution)/shard_map/all_gather | solution.py:71
  609.0 23.2 %all-gather.33.cloned.1.call-done = bf16[1,1024,2048]{2,1,0:T(8,128)(2,1)} async-done(((bf16[1,256,2048]{2,1,0:T(8,128)(2,1)}), bf16[1,1024,2048]{2,1,0:T(8,128)(2,1)}) %all-gather.33.cloned.1.call-update) | async-done | bytes 4194320 | tf_op jit(solution)/shard_map/all_gather | solution.py:227
  632.2 102.1 %all-gather.31.cloned.1.call-done = bf16[1536,2048]{1,0:T(8,128)(2,1)} async-done(((bf16[1536,256]{1,0:T(8,128)(2,1)}), bf16[1536,2048]{1,0:T(8,128)(2,1)}) %all-gather.31.cloned.1.call-update) | async-done | bytes 6291472 | tf_op jit(solution)/shard_map/all_gather | solution.py:73
  734.2 16.7 multiply_convert_fusion
  780.9 58.8 %reduce-scatter.17.cloned.1.call-done = f32[1,256,2048]{2,1,0:T(8,128)} async-done(((f32[1,1024,2048]{2,1,0:T(8,128)}), f32[1,256,2048]{2,1,0:T(8,128)}) %reduce-scatter.17.cloned.1.call-update) | async-done | bytes 2097168 | tf_op jit(solution)/shard_map/reduce_scatter | solution.py:239
  841.9 44.7 %reduce-scatter.15.cloned.1.call-done = bf16[1,256,2048]{2,1,0:T(8,128)(2,1)} async-done(((bf16[1,1024,2048]{2,1,0:T(8,128)(2,1)}), bf16[1,256,2048]{2,1,0:T(8,128)(2,1)}) %reduce-scatter.15.cloned.1.call-update) | async-done | bytes 1048592 | tf_op jit(solution)/shard_map/reduce_scatter | solution.py:207
  1051.7 118.6 %reduce-scatter.33.cloned.1.call-done = bf16[256,1536]{1,0:T(8,128)(2,1)} async-done(((bf16[2048,1536]{1,0:T(8,128)(2,1)}), bf16[256,1536]{1,0:T(8,128)(2,1)}) %reduce-scatter.33.cloned.1.call-update) | async-done | bytes 786448 | tf_op jit(solution)/shard_map/reduce_scatter | solution.py:248
  1172.8 118.5 %reduce-scatter.31.cloned.1.call-done = bf16[256,1536]{1,0:T(8,128)(2,1)} async-done(((bf16[2048,1536]{1,0:T(8,128)(2,1)}), bf16[256,1536]{1,0:T(8,128)(2,1)}) %reduce-scatter.31.cloned.1.call-update) | async-done | bytes 786448 | tf_op jit(solution)/shard_map/reduce_scatter | solution.py:245
  1293.8 63.9 %reduce-scatter.25.cloned.1.call-done = bf16[256,256]{1,0:T(8,128)(2,1)} async-done(((bf16[2048,256]{1,0:T(8,128)(2,1)}), bf16[256,256]{1,0:T(8,128)(2,1)}) %reduce-scatter.25.cloned.1.call-update) | async-done | bytes 131088 | tf_op jit(solution)/shard_map/reduce_scatter | solution.py:317
  1359.3 64.1 %reduce-scatter.23.cloned.1.call-done = bf16[256,256]{1,0:T(8,128)(2,1)} async-done(((bf16[2048,256]{1,0:T(8,128)(2,1)}), bf16[256,256]{1,0:T(8,128)(2,1)}) %reduce-scatter.23.cloned.1.call-update) | async-done | bytes 131088 | tf_op jit(solution)/shard_map/reduce_scatter | solution.py:314
  1425.1 69.7 %reduce-scatter.29.cloned.1.call-done = bf16[512,256]{1,0:T(8,128)(2,1)} async-done(((bf16[512,2048]{1,0:T(8,128)(2,1)}), bf16[512,256]{1,0:T(8,128)(2,1)}) %reduce-scatter.29.cloned.1.call-update) | async-done | bytes 262160 | tf_op jit(solution)/shard_map/reduce_scatter | solution.py:323
  1496.6 69.0 %reduce-scatter.27.cloned.1.call-done = bf16[256,512]{1,0:T(8,128)(2,1)} async-done(((bf16[2048,512]{1,0:T(8,128)(2,1)}), bf16[256,512]{1,0:T(8,128)(2,1)}) %reduce-scatter.27.cloned.1.call-update) | async-done | bytes 262160 | tf_op jit(solution)/shard_map/reduce_scatter | solution.py:320
  1567.4 69.1 %reduce-scatter.21.cloned.1.call-done = bf16[256,512]{1,0:T(8,128)(2,1)} async-done(((bf16[2048,512]{1,0:T(8,128)(2,1)}), bf16[256,512]{1,0:T(8,128)(2,1)}) %reduce-scatter.21.cloned.1.call-update) | async-done | bytes 262160 | tf_op jit(solution)/shard_map/reduce_scatter | solution.py:311
  1638.3 44.3 %reduce-scatter.19.cloned.1.call-done = bf16[1,256,2048]{2,1,0:T(8,128)(2,1)} async-done(((bf16[1,1024,2048]{2,1,0:T(8,128)(2,1)}), bf16[1,256,2048]{2,1,0:T(8,128)(2,1)}) %reduce-scatter.19.cloned.1.call-update) | async-done | bytes 1048592 | tf_op jit(solution)/shard_map/reduce_scatter | solution.py:295
  1684.4 39.8 %all-reduce = (f32[2048]{0:T(1024)}, f32[128]{0:T(128)}, f32[128]{0:T(128)}, f32[2048]{0:T(1024)}) all-reduce(f32[2048]{0:T(1024)S(1)} %get-tuple-element.57, f32[128]{0:T(128)S(1)} %bitcast_reduce_fusion, f32[128]{0:T(128)S(1)} %bitcast_reduce_fusion.1, f32[2048]{0:T(1024)S(1)} %get-tuple-element.55), channel_id=1, replica_groups=mesh['dp'=8,'ctx'=4] {'dp','ctx'}, use_global_device_ids=true, to_apply=%region_17.18 | all-reduce | flops 4352 | bytes 34816 | tf_op jit(solution)/shard_map/psum | solution.py:327
  (272 shorter events, 319.6 us)
Async XLA Ops:
  7.2 45.9 %all-gather.17.cloned.1.call-start = ((), (), s32[]{:S(2)}) async-start(), calls=%async_computation.14 | async-start | bytes 1179648 | tf_op jit(solution)/shard_map/all_gather | solution.py:62
  7.9 80.6 %all-gather.13.cloned.1.call-start = ((), (), s32[]{:S(2)}) async-start(), calls=%async_computation.12 | async-start | bytes 5242880 | tf_op jit(solution)/shard_map/all_gather | solution.py:161
  13.3 126.7 %all-gather.19.cloned.1.call-start = ((), (), s32[]{:S(2)}) async-start(), calls=%async_computation.15 | async-start | bytes 2359296 | tf_op jit(solution)/shard_map/all_gather | solution.py:61
  14.0 166.6 %all-gather.15.cloned.1.call-start = ((), (), s32[]{:S(2)}) async-start(), calls=%async_computation.13 | async-start | bytes 1179648 | tf_op jit(solution)/shard_map/all_gather | solution.py:63
  14.6 216.1 %all-gather.21.cloned.1.call-start = ((), (), s32[]{:S(2)}) async-start(), calls=%async_computation.16 | async-start | bytes 2359296 | tf_op jit(solution)/shard_map/all_gather | solution.py:64
  15.2 267.0 %all-gather.23.cloned.1.call-start = ((), (), s32[]{:S(2)}) async-start(), calls=%async_computation.17 | async-start | bytes 2359296 | tf_op jit(solution)/shard_map/all_gather | solution.py:65
  15.8 343.8 %reduce-scatter.13.cloned.1.call-start = ((), (), s32[]{:S(2)}) async-start(), calls=%async_computation.18 | async-start | bytes 10485760 | tf_op jit(solution)/shard_map/reduce_scatter | solution.py:189
  289.5 171.5 %all-gather.29.cloned.1.call-start = ((), (), s32[]{:S(2)}) async-start(), calls=%async_computation.21 | async-start | bytes 7077888 | tf_op jit(solution)/shard_map/all_gather | solution.py:72
  290.2 205.7 %all-gather.25.cloned.1.call-start = ((), (), s32[]{:S(2)}) async-start(), calls=%async_computation.19 | async-start | bytes 5242880 | tf_op jit(solution)/shard_map/all_gather | solution.py:196
  363.1 234.2 %all-gather.27.cloned.1.call-start = ((), (), s32[]{:S(2)}) async-start(), calls=%async_computation.20 | async-start | bytes 7077888 | tf_op jit(solution)/shard_map/all_gather | solution.py:71
  363.7 268.5 %all-gather.33.cloned.1.call-start = ((), (), s32[]{:S(2)}) async-start(), calls=%async_computation.24 | async-start | bytes 5242880 | tf_op jit(solution)/shard_map/all_gather | solution.py:227
  368.1 366.2 %all-gather.31.cloned.1.call-start = ((), (), s32[]{:S(2)}) async-start(), calls=%async_computation.22 | async-start | bytes 7077888 | tf_op jit(solution)/shard_map/all_gather | solution.py:73
  368.6 471.1 %reduce-scatter.17.cloned.1.call-start = ((), (), s32[]{:S(2)}) async-start(), calls=%async_computation.25 | async-start | bytes 10485760 | tf_op jit(solution)/shard_map/reduce_scatter | solution.py:239
  769.6 117.0 %reduce-scatter.15.cloned.1.call-start = ((), (), s32[]{:S(2)}) async-start(), calls=%async_computation.23 | async-start | bytes 5242880 | tf_op jit(solution)/shard_map/reduce_scatter | solution.py:207
  780.8 146.9 %all-gather.35.cloned.1.call-start = ((), (), s32[]{:S(2)}) async-start(), calls=%async_computation.26 | async-start | bytes 5242880 | tf_op jit(solution)/shard_map/all_gather | solution.py:257
  892.4 157.0 %reduce-scatter.35.cloned.1.call-start = ((), (), s32[]{:S(2)}) async-start(), calls=%async_computation.35 | async-start | bytes 7077888 | tf_op jit(solution)/shard_map/reduce_scatter | solution.py:251
  904.0 266.3 %reduce-scatter.33.cloned.1.call-start = ((), (), s32[]{:S(2)}) async-start(), calls=%async_computation.34 | async-start | bytes 7077888 | tf_op jit(solution)/shard_map/reduce_scatter | solution.py:248
  915.5 375.8 %reduce-scatter.31.cloned.1.call-start = ((), (), s32[]{:S(2)}) async-start(), calls=%async_computation.33 | async-start | bytes 7077888 | tf_op jit(solution)/shard_map/reduce_scatter | solution.py:245
  927.1 430.6 %reduce-scatter.25.cloned.1.call-start = ((), (), s32[]{:S(2)}) async-start(), calls=%async_computation.30 | async-start | bytes 1179648 | tf_op jit(solution)/shard_map/reduce_scatter | solution.py:317
  958.7 464.8 %reduce-scatter.23.cloned.1.call-start = ((), (), s32[]{:S(2)}) async-start(), calls=%async_computation.29 | async-start | bytes 1179648 | tf_op jit(solution)/shard_map/reduce_scatter | solution.py:314
  985.0 509.8 %reduce-scatter.29.cloned.1.call-start = ((), (), s32[]{:S(2)}) async-start(), calls=%async_computation.32 | async-start | bytes 2359296 | tf_op jit(solution)/shard_map/reduce_scatter | solution.py:323
  991.0 574.6 %reduce-scatter.27.cloned.1.call-start = ((), (), s32[]{:S(2)}) async-start(), calls=%async_computation.31 | async-start | bytes 2359296 | tf_op jit(solution)/shard_map/reduce_scatter | solution.py:320
  997.5 639.0 %reduce-scatter.21.cloned.1.call-start = ((), (), s32[]{:S(2)}) async-start(), calls=%async_computation.28 | async-start | bytes 2359296 | tf_op jit(solution)/shard_map/reduce_scatter | solution.py:311
  1011.6 670.9 %reduce-scatter.19.cloned.1.call-start = ((), (), s32[]{:S(2)}) async-start(), calls=%async_computation.27 | async-start | bytes 5242880 | tf_op jit(solution)/shard_map/reduce_scatter | solution.py:295
  (67 other events, 3181.3 us)
Sparse Core Ops, SparseCore 0:
  10.1 42.9 all-gather.16
  55.2 33.2 all-gather.12
  90.6 49.2 all-gather.18
  141.9 38.6 all-gather.14
  182.6 48.0 all-gather.20
  232.6 49.5 all-gather.22
  289.6 69.8 reduce-scatter.12
  361.9 99.0 all-gather.28
  463.2 32.6 all-gather.24
  498.2 99.0 all-gather.26
  599.5 32.6 all-gather.32
  634.3 99.9 all-gather.30
  769.8 69.9 reduce-scatter.16
  842.1 44.4 reduce-scatter.14
  892.5 34.4 all-gather.34
  930.9 118.3 reduce-scatter.34
  1053.2 117.0 reduce-scatter.32
  1174.2 117.0 reduce-scatter.30
  1295.1 62.5 reduce-scatter.24
  1361.0 62.4 reduce-scatter.22
  1427.4 67.3 reduce-scatter.28
  1498.7 66.7 reduce-scatter.26
  1569.5 66.9 reduce-scatter.20
  1639.0 43.4 reduce-scatter.18
where the time goes:
time: 1740 us; the launch traced here: 1730 us
  waiting for transfers between devices  1360 us (78%)
  matrix products  228 us (13%)
  other arithmetic  73.9 us (4%)
  blocking collectives  39.8 us (2%)
    reduce_scatter x1, waiting for transfers between devices, per_device(): lax.psum_scatter(grad_up.astype(jnp.bfloat16), 'dp', scatter_dimension=0,...  119 us
    reduce_scatter x1, waiting for transfers between devices, per_device(): lax.psum_scatter(grad_gate.astype(jnp.bfloat16), 'dp', scatter_dimension=...  119 us
    all_gather x1, waiting for transfers between devices, swiglu_weights(): lax.all_gather(swiglu_down, 'dp', axis=1, tiled=True)  102 us
    all_gather x1, waiting for transfers between devices, swiglu_weights(): lax.all_gather(swiglu_up, 'dp', axis=0, tiled=True)  92.3 us
    all_gather x1, waiting for transfers between devices, swiglu_weights(): lax.all_gather(swiglu_gate, 'dp', axis=0, tiled=True)  89.6 us
    reduce_scatter x1, waiting for transfers between devices, per_device(): lax.psum_scatter(grad_output.astype(jnp.bfloat16), 'dp', scatter_dimensio...  69.7 us
    reduce_scatter x1, waiting for transfers between devices, per_device(): lax.psum_scatter(branch_part, 'ctx', scatter_dimension=1, tiled=True)  69.2 us
    reduce_scatter x1, waiting for transfers between devices, per_device(): lax.psum_scatter(grad_query.astype(jnp.bfloat16), 'dp', scatter_dimension...  69.1 us
  transfers between devices with their start and end apart: 24, of which 23 were waited for; matrix products, arithmetic and copies ran while one was open for 15% of the time, Pallas kernels for 0%

commit v1 on v0

--- a/solution.py
+++ b/solution.py
@@ -325,7 +325,7 @@
         ).astype(jnp.float32),
     )
     gain_grads = lax.psum(
-        (grad_gain_in, grad_gain_mid, grad_query_gain, grad_key_gain), ("dp", "ctx")
+        lax.psum((grad_gain_in, grad_gain_mid, grad_query_gain, grad_key_gain), "dp"), "ctx"
     )
     return (
         layer_out.reshape(seq_count, local_len, model_width),

time: 1740 us -> 1750 us (level)
    psum x1 -> x2, blocking collectives: 39.8 us -> 48 us  [the longest x1 37.1 us: per_device(): lax.psum((grad_gain_in, grad_gain_mid, grad_query_gain, grad_key_gain), '...]
where the time goes in v1:
time: 1750 us; the launch traced here: 1740 us
  waiting for transfers between devices  1360 us (78%)
  matrix products  228 us (13%)
  other arithmetic  73.9 us (4%)
  blocking collectives  48 us (3%)
    reduce_scatter x1, waiting for transfers between devices, per_device(): lax.psum_scatter(grad_up.astype(jnp.bfloat16), 'dp', scatter_dimension=0,...  119 us
    reduce_scatter x1, waiting for transfers between devices, per_device(): lax.psum_scatter(grad_gate.astype(jnp.bfloat16), 'dp', scatter_dimension=...  119 us
    all_gather x1, waiting for transfers between devices, swiglu_weights(): lax.all_gather(swiglu_down, 'dp', axis=1, tiled=True)  102 us
    all_gather x1, waiting for transfers between devices, swiglu_weights(): lax.all_gather(swiglu_up, 'dp', axis=0, tiled=True)  92.3 us
    all_gather x1, waiting for transfers between devices, swiglu_weights(): lax.all_gather(swiglu_gate, 'dp', axis=0, tiled=True)  89.5 us
    reduce_scatter x1, waiting for transfers between devices, per_device(): lax.psum_scatter(grad_output.astype(jnp.bfloat16), 'dp', scatter_dimensio...  69.7 us
    reduce_scatter x1, waiting for transfers between devices, per_device(): lax.psum_scatter(branch_part, 'ctx', scatter_dimension=1, tiled=True)  69.2 us
    reduce_scatter x1, waiting for transfers between devices, per_device(): lax.psum_scatter(grad_gating.astype(jnp.bfloat16), 'dp', scatter_dimensio...  69.1 us
  transfers between devices with their start and end apart: 24, of which 23 were waited for; matrix products, arithmetic and copies ran while one was open for 15% of the time, Pallas kernels for 0%

profile of v1, /device:TPU:0, one launch (start us, length us, event | category | flops | bytes accessed | tf_op | source)
XLA Modules:
  0.0 1742.8 jit_solution(16299189281773648647)
XLA Ops:
  18.6 34.5 %all-gather.17.cloned.1.call-done = bf16[2048,256]{1,0:T(8,128)(2,1)} async-done(((bf16[256,256]{1,0:T(8,128)(2,1)}), bf16[2048,256]{1,0:T(8,128)(2,1)}) %all-gather.17.cloned.1.call-update) | async-done | bytes 1048592 | tf_op jit(solution)/shard_map/all_gather | solution.py:62
  53.1 35.4 %all-gather.13.cloned.1.call-done = bf16[1,1024,2048]{2,1,0:T(8,128)(2,1)} async-done(((bf16[1,256,2048]{2,1,0:T(8,128)(2,1)}), bf16[1,1024,2048]{2,1,0:T(8,128)(2,1)}) %all-gather.13.cloned.1.call-update) | async-done | bytes 4194320 | tf_op jit(solution)/shard_map/all_gather | solution.py:161
  93.4 46.5 %all-gather.19.cloned.1.call-done = bf16[2048,512]{1,0:T(8,128)(2,1)} async-done(((bf16[256,512]{1,0:T(8,128)(2,1)}), bf16[2048,512]{1,0:T(8,128)(2,1)}) %all-gather.19.cloned.1.call-update) | async-done | bytes 2097168 | tf_op jit(solution)/shard_map/all_gather | solution.py:61
  162.0 18.6 %all-gather.15.cloned.1.call-done = bf16[2048,256]{1,0:T(8,128)(2,1)} async-done(((bf16[256,256]{1,0:T(8,128)(2,1)}), bf16[2048,256]{1,0:T(8,128)(2,1)}) %all-gather.15.cloned.1.call-update) | async-done | bytes 1048592 | tf_op jit(solution)/shard_map/all_gather | solution.py:63
  200.4 30.4 %all-gather.21.cloned.1.call-done = bf16[2048,512]{1,0:T(8,128)(2,1)} async-done(((bf16[256,512]{1,0:T(8,128)(2,1)}), bf16[2048,512]{1,0:T(8,128)(2,1)}) %all-gather.21.cloned.1.call-update) | async-done | bytes 2097168 | tf_op jit(solution)/shard_map/all_gather | solution.py:64
  237.7 44.6 %all-gather.23.cloned.1.call-done = bf16[512,2048]{1,0:T(8,128)(2,1)} async-done(((bf16[512,256]{1,0:T(8,128)(2,1)}), bf16[512,2048]{1,0:T(8,128)(2,1)}) %all-gather.23.cloned.1.call-update) | async-done | bytes 2097168 | tf_op jit(solution)/shard_map/all_gather | solution.py:65
  290.5 69.2 %reduce-scatter.13.cloned.1.call-done = f32[1,256,2048]{2,1,0:T(8,128)} async-done(((f32[1,1024,2048]{2,1,0:T(8,128)}), f32[1,256,2048]{2,1,0:T(8,128)}) %reduce-scatter.13.cloned.1.call-update) | async-done | bytes 2097168 | tf_op jit(solution)/shard_map/reduce_scatter | solution.py:189
  368.8 92.3 %all-gather.29.cloned.1.call-done = bf16[2048,1536]{1,0:T(8,128)(2,1)} async-done(((bf16[256,1536]{1,0:T(8,128)(2,1)}), bf16[2048,1536]{1,0:T(8,128)(2,1)}) %all-gather.29.cloned.1.call-update) | async-done | bytes 6291472 | tf_op jit(solution)/shard_map/all_gather | solution.py:72
  461.2 34.9 %all-gather.25.cloned.1.call-done = bf16[1,1024,2048]{2,1,0:T(8,128)(2,1)} async-done(((bf16[1,256,2048]{2,1,0:T(8,128)(2,1)}), bf16[1,1024,2048]{2,1,0:T(8,128)(2,1)}) %all-gather.25.cloned.1.call-update) | async-done | bytes 4194320 | tf_op jit(solution)/shard_map/all_gather | solution.py:196
  507.9 89.5 %all-gather.27.cloned.1.call-done = bf16[2048,1536]{1,0:T(8,128)(2,1)} async-done(((bf16[256,1536]{1,0:T(8,128)(2,1)}), bf16[2048,1536]{1,0:T(8,128)(2,1)}) %all-gather.27.cloned.1.call-update) | async-done | bytes 6291472 | tf_op jit(solution)/shard_map/all_gather | solution.py:71
  609.1 23.2 %all-gather.33.cloned.1.call-done = bf16[1,1024,2048]{2,1,0:T(8,128)(2,1)} async-done(((bf16[1,256,2048]{2,1,0:T(8,128)(2,1)}), bf16[1,1024,2048]{2,1,0:T(8,128)(2,1)}) %all-gather.33.cloned.1.call-update) | async-done | bytes 4194320 | tf_op jit(solution)/shard_map/all_gather | solution.py:227
  632.3 102.1 %all-gather.31.cloned.1.call-done = bf16[1536,2048]{1,0:T(8,128)(2,1)} async-done(((bf16[1536,256]{1,0:T(8,128)(2,1)}), bf16[1536,2048]{1,0:T(8,128)(2,1)}) %all-gather.31.cloned.1.call-update) | async-done | bytes 6291472 | tf_op jit(solution)/shard_map/all_gather | solution.py:73
  734.4 16.9 multiply_convert_fusion
  781.2 58.8 %reduce-scatter.17.cloned.1.call-done = f32[1,256,2048]{2,1,0:T(8,128)} async-done(((f32[1,1024,2048]{2,1,0:T(8,128)}), f32[1,256,2048]{2,1,0:T(8,128)}) %reduce-scatter.17.cloned.1.call-update) | async-done | bytes 2097168 | tf_op jit(solution)/shard_map/reduce_scatter | solution.py:239
  842.2 44.7 %reduce-scatter.15.cloned.1.call-done = bf16[1,256,2048]{2,1,0:T(8,128)(2,1)} async-done(((bf16[1,1024,2048]{2,1,0:T(8,128)(2,1)}), bf16[1,256,2048]{2,1,0:T(8,128)(2,1)}) %reduce-scatter.15.cloned.1.call-update) | async-done | bytes 1048592 | tf_op jit(solution)/shard_map/reduce_scatter | solution.py:207
  1052.0 118.6 %reduce-scatter.33.cloned.1.call-done = bf16[256,1536]{1,0:T(8,128)(2,1)} async-done(((bf16[2048,1536]{1,0:T(8,128)(2,1)}), bf16[256,1536]{1,0:T(8,128)(2,1)}) %reduce-scatter.33.cloned.1.call-update) | async-done | bytes 786448 | tf_op jit(solution)/shard_map/reduce_scatter | solution.py:248
  1173.1 118.6 %reduce-scatter.31.cloned.1.call-done = bf16[256,1536]{1,0:T(8,128)(2,1)} async-done(((bf16[2048,1536]{1,0:T(8,128)(2,1)}), bf16[256,1536]{1,0:T(8,128)(2,1)}) %reduce-scatter.31.cloned.1.call-update) | async-done | bytes 786448 | tf_op jit(solution)/shard_map/reduce_scatter | solution.py:245
  1294.2 64.0 %reduce-scatter.25.cloned.1.call-done = bf16[256,256]{1,0:T(8,128)(2,1)} async-done(((bf16[2048,256]{1,0:T(8,128)(2,1)}), bf16[256,256]{1,0:T(8,128)(2,1)}) %reduce-scatter.25.cloned.1.call-update) | async-done | bytes 131088 | tf_op jit(solution)/shard_map/reduce_scatter | solution.py:317
  1359.8 64.1 %reduce-scatter.23.cloned.1.call-done = bf16[256,256]{1,0:T(8,128)(2,1)} async-done(((bf16[2048,256]{1,0:T(8,128)(2,1)}), bf16[256,256]{1,0:T(8,128)(2,1)}) %reduce-scatter.23.cloned.1.call-update) | async-done | bytes 131088 | tf_op jit(solution)/shard_map/reduce_scatter | solution.py:314
  1425.5 69.7 %reduce-scatter.29.cloned.1.call-done = bf16[512,256]{1,0:T(8,128)(2,1)} async-done(((bf16[512,2048]{1,0:T(8,128)(2,1)}), bf16[512,256]{1,0:T(8,128)(2,1)}) %reduce-scatter.29.cloned.1.call-update) | async-done | bytes 262160 | tf_op jit(solution)/shard_map/reduce_scatter | solution.py:323
  1497.0 69.1 %reduce-scatter.27.cloned.1.call-done = bf16[256,512]{1,0:T(8,128)(2,1)} async-done(((bf16[2048,512]{1,0:T(8,128)(2,1)}), bf16[256,512]{1,0:T(8,128)(2,1)}) %reduce-scatter.27.cloned.1.call-update) | async-done | bytes 262160 | tf_op jit(solution)/shard_map/reduce_scatter | solution.py:320
  1567.9 69.1 %reduce-scatter.21.cloned.1.call-done = bf16[256,512]{1,0:T(8,128)(2,1)} async-done(((bf16[2048,512]{1,0:T(8,128)(2,1)}), bf16[256,512]{1,0:T(8,128)(2,1)}) %reduce-scatter.21.cloned.1.call-update) | async-done | bytes 262160 | tf_op jit(solution)/shard_map/reduce_scatter | solution.py:311
  1638.8 44.2 %reduce-scatter.19.cloned.1.call-done = bf16[1,256,2048]{2,1,0:T(8,128)(2,1)} async-done(((bf16[1,1024,2048]{2,1,0:T(8,128)(2,1)}), bf16[1,256,2048]{2,1,0:T(8,128)(2,1)}) %reduce-scatter.19.cloned.1.call-update) | async-done | bytes 1048592 | tf_op jit(solution)/shard_map/reduce_scatter | solution.py:295
  1684.9 37.1 %all-reduce = (f32[2048]{0:T(1024)S(1)}, f32[128]{0:T(128)S(1)}, f32[128]{0:T(128)S(1)}, f32[2048]{0:T(1024)S(1)}) all-reduce(f32[2048]{0:T(1024)S(1)} %get-tuple-element.57, f32[128]{0:T(128)S(1)} %bitcast_reduce_fusion, f32[128]{0:T(128)S(1)} %bitcast_reduce_fusion.1, ...), channel_id=1, replica_groups=mesh['dp'=8,'ctx'=4] {'dp'}, use_global_device_ids=true, to_apply=%region_17.18 | all-reduce | flops 4352 | bytes 34816 | tf_op jit(solution)/shard_map/psum | solution.py:328
  (273 shorter events, 330.6 us)
Async XLA Ops:
  7.2 45.9 %all-gather.17.cloned.1.call-start = ((), (), s32[]{:S(2)}) async-start(), calls=%async_computation.14 | async-start | bytes 1179648 | tf_op jit(solution)/shard_map/all_gather | solution.py:62
  7.9 80.6 %all-gather.13.cloned.1.call-start = ((), (), s32[]{:S(2)}) async-start(), calls=%async_computation.12 | async-start | bytes 5242880 | tf_op jit(solution)/shard_map/all_gather | solution.py:161
  13.3 126.7 %all-gather.19.cloned.1.call-start = ((), (), s32[]{:S(2)}) async-start(), calls=%async_computation.15 | async-start | bytes 2359296 | tf_op jit(solution)/shard_map/all_gather | solution.py:61
  14.0 166.6 %all-gather.15.cloned.1.call-start = ((), (), s32[]{:S(2)}) async-start(), calls=%async_computation.13 | async-start | bytes 1179648 | tf_op jit(solution)/shard_map/all_gather | solution.py:63
  14.6 216.2 %all-gather.21.cloned.1.call-start = ((), (), s32[]{:S(2)}) async-start(), calls=%async_computation.16 | async-start | bytes 2359296 | tf_op jit(solution)/shard_map/all_gather | solution.py:64
  15.2 267.1 %all-gather.23.cloned.1.call-start = ((), (), s32[]{:S(2)}) async-start(), calls=%async_computation.17 | async-start | bytes 2359296 | tf_op jit(solution)/shard_map/all_gather | solution.py:65
  15.8 343.9 %reduce-scatter.13.cloned.1.call-start = ((), (), s32[]{:S(2)}) async-start(), calls=%async_computation.18 | async-start | bytes 10485760 | tf_op jit(solution)/shard_map/reduce_scatter | solution.py:189
  289.6 171.5 %all-gather.29.cloned.1.call-start = ((), (), s32[]{:S(2)}) async-start(), calls=%async_computation.21 | async-start | bytes 7077888 | tf_op jit(solution)/shard_map/all_gather | solution.py:72
  290.4 205.7 %all-gather.25.cloned.1.call-start = ((), (), s32[]{:S(2)}) async-start(), calls=%async_computation.19 | async-start | bytes 5242880 | tf_op jit(solution)/shard_map/all_gather | solution.py:196
  363.2 234.2 %all-gather.27.cloned.1.call-start = ((), (), s32[]{:S(2)}) async-start(), calls=%async_computation.20 | async-start | bytes 7077888 | tf_op jit(solution)/shard_map/all_gather | solution.py:71
  363.8 268.5 %all-gather.33.cloned.1.call-start = ((), (), s32[]{:S(2)}) async-start(), calls=%async_computation.24 | async-start | bytes 5242880 | tf_op jit(solution)/shard_map/all_gather | solution.py:227
  368.2 366.2 %all-gather.31.cloned.1.call-start = ((), (), s32[]{:S(2)}) async-start(), calls=%async_computation.22 | async-start | bytes 7077888 | tf_op jit(solution)/shard_map/all_gather | solution.py:73
  368.8 471.2 %reduce-scatter.17.cloned.1.call-start = ((), (), s32[]{:S(2)}) async-start(), calls=%async_computation.25 | async-start | bytes 10485760 | tf_op jit(solution)/shard_map/reduce_scatter | solution.py:239
  769.9 117.0 %reduce-scatter.15.cloned.1.call-start = ((), (), s32[]{:S(2)}) async-start(), calls=%async_computation.23 | async-start | bytes 5242880 | tf_op jit(solution)/shard_map/reduce_scatter | solution.py:207
  781.1 146.9 %all-gather.35.cloned.1.call-start = ((), (), s32[]{:S(2)}) async-start(), calls=%async_computation.26 | async-start | bytes 5242880 | tf_op jit(solution)/shard_map/all_gather | solution.py:257
  892.7 157.0 %reduce-scatter.35.cloned.1.call-start = ((), (), s32[]{:S(2)}) async-start(), calls=%async_computation.35 | async-start | bytes 7077888 | tf_op jit(solution)/shard_map/reduce_scatter | solution.py:251
  904.3 266.4 %reduce-scatter.33.cloned.1.call-start = ((), (), s32[]{:S(2)}) async-start(), calls=%async_computation.34 | async-start | bytes 7077888 | tf_op jit(solution)/shard_map/reduce_scatter | solution.py:248
  915.9 375.8 %reduce-scatter.31.cloned.1.call-start = ((), (), s32[]{:S(2)}) async-start(), calls=%async_computation.33 | async-start | bytes 7077888 | tf_op jit(solution)/shard_map/reduce_scatter | solution.py:245
  927.4 430.8 %reduce-scatter.25.cloned.1.call-start = ((), (), s32[]{:S(2)}) async-start(), calls=%async_computation.30 | async-start | bytes 1179648 | tf_op jit(solution)/shard_map/reduce_scatter | solution.py:317
  959.0 464.8 %reduce-scatter.23.cloned.1.call-start = ((), (), s32[]{:S(2)}) async-start(), calls=%async_computation.29 | async-start | bytes 1179648 | tf_op jit(solution)/shard_map/reduce_scatter | solution.py:314
  985.6 509.6 %reduce-scatter.29.cloned.1.call-start = ((), (), s32[]{:S(2)}) async-start(), calls=%async_computation.32 | async-start | bytes 2359296 | tf_op jit(solution)/shard_map/reduce_scatter | solution.py:323
  991.6 574.5 %reduce-scatter.27.cloned.1.call-start = ((), (), s32[]{:S(2)}) async-start(), calls=%async_computation.31 | async-start | bytes 2359296 | tf_op jit(solution)/shard_map/reduce_scatter | solution.py:320
  998.2 638.8 %reduce-scatter.21.cloned.1.call-start = ((), (), s32[]{:S(2)}) async-start(), calls=%async_computation.28 | async-start | bytes 2359296 | tf_op jit(solution)/shard_map/reduce_scatter | solution.py:311
  1012.2 670.8 %reduce-scatter.19.cloned.1.call-start = ((), (), s32[]{:S(2)}) async-start(), calls=%async_computation.27 | async-start | bytes 5242880 | tf_op jit(solution)/shard_map/reduce_scatter | solution.py:295
  (67 other events, 3198.5 us)
Sparse Core Ops, SparseCore 0:
  10.1 42.9 all-gather.16
  55.2 33.2 all-gather.12
  90.6 49.2 all-gather.18
  141.9 38.6 all-gather.14
  182.6 48.1 all-gather.20
  232.7 49.5 all-gather.22
  289.8 69.8 reduce-scatter.12
  362.1 99.0 all-gather.28
  463.4 32.6 all-gather.24
  498.3 99.0 all-gather.26
  599.6 32.6 all-gather.32
  634.4 99.9 all-gather.30
  770.0 69.9 reduce-scatter.16
  842.4 44.4 reduce-scatter.14
  892.8 34.4 all-gather.34
  931.2 118.3 reduce-scatter.34
  1053.5 117.1 reduce-scatter.32
  1174.5 117.1 reduce-scatter.30
  1295.5 62.6 reduce-scatter.24
  1361.4 62.4 reduce-scatter.22
  1427.8 67.3 reduce-scatter.28
  1499.2 66.9 reduce-scatter.26
  1570.1 66.8 reduce-scatter.20
  1639.6 43.4 reduce-scatter.18
